TPU v7x, 256 devices: a whole 4x4x8 slice. The times are simulated.
256 devices in a mesh: row: 32 (over z, x), src: 8 (over y, core).
Axes of the slice: x: 4, y: 4, z: 8, core: 2. Of those that a mesh axis runs over, the one named last changes fastest.
Arguments:
- sub_source: float32 [32768, 4096], P('row', 'src'), may hold values from -6 to 6
- sub_inverse: bfloat16 [32768, 1024], P('row'), as said below
- coupling: bfloat16 [32, 2, 512, 1024], P('row'), may hold values from -0.0625 to 0.0625
- update_lists: int32 [32, 2], P('row'), may hold values from 0 to 3, as said below
- sep_source: float32 [2048, 4096], P('row', 'src'), may hold values from -6 to 6
- sep_inverse: bfloat16 [16384, 512], P(('row', 'src')), as said below
- sep_lower: bfloat16 [16384, 1024], P(('row', 'src')), may hold values from -0.125 to 0.125
- factor_owner_slots: int32 [4], replicated, may hold values from 0 to 31, as said below
- sep_links: int32 [4, 2], replicated, may hold values from -1 to 2, as said below
Outputs:
- sub_field: float32 [32768, 4096], P('row', 'src')
- sep_field: float32 [2048, 4096], P('row', 'src')
Inputs may be any that keep to these rules, and one draw needn't show every extreme that they name: `update_lists`: each subtree lists two different separator blocks. `factor_owner_slots`: the 4 entries are different slots. `sep_links`: for block k the first entry is k - 1 and the second is -1 or a block below k - 1; -1 means no link. `sub_inverse`: each slot of 1024 rows is lower triangular. `sep_inverse`: each slot of 512 rows is lower triangular.
All inputs are finite; a program needn't handle non-finite values.
Results may differ from a plain program's by a relative error of at most 0.006.
Values may be sent and summed in bfloat16 or wider, within the bound.
A program may use at most 64 MiB of HBM per device.

v0:
```python
import jax
import jax.numpy as jnp
from jax import lax
from jax.sharding import PartitionSpec as P

SEP_BLOCK = 512
STEPS = 4
LINKS = 2
SEP_ROWS = 2048


def from_root(shard, axis, root):
    mine = lax.axis_index(axis) == root
    return lax.psum(jnp.where(mine, shard, jnp.zeros_like(shard)), axis)


def per_device(
    sub_source,
    sub_inverse,
    coupling,
    update_lists,
    sep_source,
    sep_inverse,
    sep_lower,
    factor_owner_slots,
    sep_links,
):
    sources = sub_source.shape[1]
    sub_field = jnp.dot(
        sub_inverse, sub_source.astype(jnp.bfloat16), preferred_element_type=jnp.float32
    )
    padded_length = sub_field.astype(jnp.bfloat16)
    pending_updates = jnp.einsum(
        "rmf,ft->rmt", coupling[0], padded_length, preferred_element_type=jnp.float32
    )
    picks = update_lists[0][:, None] == jnp.arange(STEPS, dtype=jnp.int32)[None, :]
    dense = jnp.sum(jnp.where(picks[:, :, None, None], pending_updates[:, None], 0.0), axis=0)
    local_rows = sep_source.shape[0]
    my_row = lax.axis_index("row")
    placed = lax.dynamic_update_slice(
        jnp.zeros((SEP_ROWS, sources), jnp.float32),
        sep_source,
        (my_row * local_rows, jnp.zeros((), jnp.int32)),
    )
    terms = placed - dense.reshape(SEP_ROWS, sources)
    totals = lax.psum(terms, "row")
    inverse_row_block, lower_rows = (
        lax.all_gather(sep_inverse, "src", axis=0, tiled=True),
        lax.all_gather(sep_lower, "src", axis=0, tiled=True),
    )
    solved = jnp.zeros((STEPS, SEP_BLOCK, sources), jnp.float32)
    for block_id in range(STEPS):
        pending = totals[block_id * SEP_BLOCK : (block_id + 1) * SEP_BLOCK]
        pieces = []
        for link_pos in range(LINKS):
            target = sep_links[block_id, link_pos]
            chosen = solved[jnp.maximum(target, 0)]
            pieces.append(jnp.where(target >= 0, chosen, 0.0).astype(jnp.bfloat16))
        stacked = jnp.concatenate(pieces, axis=0)
        remaining_source = pending - jnp.dot(
            lower_rows, stacked, preferred_element_type=jnp.float32
        )
        candidate = jnp.dot(
            inverse_row_block,
            remaining_source.astype(jnp.bfloat16),
            preferred_element_type=jnp.float32,
        )
        result = from_root(candidate, "row", factor_owner_slots[block_id])
        solved = solved.at[block_id].set(result)
    whole_field = solved.reshape(SEP_ROWS, sources)
    own_rows = lax.dynamic_slice_in_dim(whole_field, my_row * local_rows, local_rows, 0)
    return (sub_field, own_rows)


def solution(mesh):
    return jax.shard_map(
        per_device,
        mesh=mesh,
        in_specs=(
            P("row", "src"),
            P("row", None),
            P("row", None, None, None),
            P("row", None),
            P("row", "src"),
            P(("row", "src"), None),
            P(("row", "src"), None),
            P(),
            P(),
        ),
        out_specs=(P("row", "src"), P("row", "src")),
        check_vma=False,
    )
```

profile of v0, /device:TPU:8, one launch (start us, length us, event | category | flops | bytes accessed | tf_op | source)
XLA Modules:
  0.0 840.7 jit_solution(14617722687658571348)
XLA Ops:
  8.0 0.0 copy-start
  8.0 0.0 all-gather.2.cloned.1.call-start
  8.1 0.7 all-gather.2.cloned.1.call-update
  8.7 0.0 all-reduce.8.cloned.1.call-start
  8.8 1.0 copy.16
  9.8 0.0 copy-done
  9.8 0.0 copy-start.6
  9.9 3.0 fusion.32
  12.8 0.0 copy-start.8
  12.9 1.3 copy-done.8
  14.2 0.0 copy-done.6
  14.2 0.0 copy-start.7
  14.2 2.6 fusion.2
  16.8 2.9 copy.18
  19.7 0.0 copy-done.7
  19.7 0.1 iota_compare_fusion
  19.8 4.9 select_reduce_fusion
  24.7 5.4 copy.23
  30.1 2.5 broadcast_in_dim.36
  32.6 1.8 dynamic_update_slice.3
  34.4 6.7 sub.15
  41.1 0.0 copy-start.5
  41.1 0.0 copy-start.3
  41.1 0.0 all-reduce.8.cloned.1.call-update
  41.1 0.0 copy-start.4
  41.1 0.0 all-reduce.10.cloned.1.call-start
  41.2 0.6 copy-done.5
  41.7 0.7 fusion.55
  43.1 0.0 copy-done.3
  43.1 13.3 %all_gather.7 = bf16[512,512]{1,0:T(8,128)(2,1)S(1)} all-gather(bf16[64,512]{1,0:T(8,128)(2,1)S(1)} %copy-done.3), channel_id=1, replica_groups=mesh['row'=32,'src'=8] {'src'}, dimensions={0}, use_global_device_ids=true | all-gather | bytes 589824 | tf_op jit(solution)/shard_map/all_gather | solution.py:48
  56.4 0.0 copy-start.2
  56.4 0.0 all-gather.2.cloned.1.call-done
  56.4 152.0 %all-reduce.8.cloned.1.call-done = f32[2048,512]{0,1:T(8,128)} async-done(((f32[2048,512]{0,1:T(8,128)}), f32[2048,512]{0,1:T(8,128)}) %all-reduce.8.cloned.1.call-update) | async-done | bytes 4194320 | tf_op jit(solution)/shard_map/psum | solution.py:46
  208.4 3.8 fusion.8
  212.2 0.0 all-reduce.10.cloned.1.call-update
  212.2 0.0 all-reduce.12.cloned.1.call-start
  212.3 0.0 copy-done.4
  212.3 0.7 fusion.54
  215.9 143.8 %all-reduce.10.cloned.1.call-done = f32[1,512,512]{1,2,0:T(8,128)} async-done(((f32[1,512,512]{1,2,0:T(8,128)}), f32[1,512,512]{1,2,0:T(8,128)}) %all-reduce.10.cloned.1.call-update) | async-done | bytes 1048592 | tf_op jit(solution)/shard_map/psum | solution.py:14
  359.7 0.0 copy-done.2
  359.7 0.0 copy-start.1
  359.7 2.7 fusion.45
  362.5 4.0 fusion.7
  366.4 0.0 all-reduce.12.cloned.1.call-update
  366.5 0.0 all-reduce.14.cloned.1.call-start
  369.7 0.0 copy-done.1
  369.7 2.6 scatter.14
  372.3 141.5 %all-reduce.12.cloned.1.call-done = f32[1,512,512]{1,2,0:T(8,128)} async-done(((f32[1,512,512]{1,2,0:T(8,128)}), f32[1,512,512]{1,2,0:T(8,128)}) %all-reduce.12.cloned.1.call-update) | async-done | bytes 1048592 | tf_op jit(solution)/shard_map/psum | solution.py:14
  513.8 2.3 constant_dynamic-update-slice_fusion.2
  516.1 1.8 fusion.40
  517.9 3.7 fusion.6
  521.5 0.0 all-reduce.14.cloned.1.call-update
  521.6 0.0 all-reduce.16.cloned.1.call-start
  524.7 144.2 %all-reduce.14.cloned.1.call-done = f32[1,512,512]{1,2,0:T(8,128)} async-done(((f32[1,512,512]{1,2,0:T(8,128)}), f32[1,512,512]{1,2,0:T(8,128)}) %all-reduce.14.cloned.1.call-update) | async-done | bytes 1048592 | tf_op jit(solution)/shard_map/psum | solution.py:14
  668.9 2.3 constant_dynamic-update-slice_fusion.1
  671.2 1.8 fusion.42
  673.0 3.7 fusion.5
  676.7 0.0 all-reduce.16.cloned.1.call-update
  676.7 147.3 %all-reduce.16.cloned.1.call-done = f32[1,512,512]{1,2,0:T(8,128)} async-done(((f32[1,512,512]{1,2,0:T(8,128)}), f32[1,512,512]{1,2,0:T(8,128)}) %all-reduce.16.cloned.1.call-update) | async-done | bytes 1048592 | tf_op jit(solution)/shard_map/psum | solution.py:14
  824.1 2.3 constant_dynamic-update-slice_fusion
  826.3 5.2 copy.20
  831.6 1.6 constant_dynamic-slice_fusion
  (2 shorter events, 0.0 us)
Async XLA Ops:
  8.0 1.8 copy-start
  8.0 48.4 %all-gather.2.cloned.1.call-start = ((), (), s32[]{:S(2)}) async-start(), calls=%async_computation.1 | async-start | bytes 1179648 | tf_op jit(solution)/shard_map/all_gather | solution.py:49
  8.7 199.7 %all-reduce.8.cloned.1.call-start = ((), (), s32[]{:S(2)}) async-start(), calls=%async_computation | async-start | bytes 8388608 | tf_op jit(solution)/shard_map/psum | solution.py:46
  9.8 4.3 copy-start.6
  12.8 1.3 copy-start.8
  14.2 5.6 copy-start.7
  41.1 0.7 copy-start.5
  41.1 2.0 copy-start.3
  41.1 171.2 %copy-start.4 = (s32[4,2]{0,1:T(2,128)S(1)}, s32[4,2]{0,1:T(2,128)}, u32[]{:S(2)}) copy-start(s32[4,2]{0,1:T(2,128)} %param.25) | copy-start | bytes 100
  41.1 318.6 %all-reduce.10.cloned.1.call-start = ((), (), s32[]{:S(2)}) async-start(), calls=%async_computation.2 | async-start | bytes 2097152 | tf_op jit(solution)/shard_map/psum | solution.py:14
  56.4 303.3 %copy-start.2 = (bf16[512,512]{1,0:T(8,128)(2,1)}, bf16[512,512]{1,0:T(8,128)(2,1)S(1)}, u32[]{:S(2)}) copy-start(bf16[512,512]{1,0:T(8,128)(2,1)S(1)} %all_gather.7) | copy-start | bytes 1572868
  212.2 301.6 %all-reduce.12.cloned.1.call-start = ((), (), s32[]{:S(2)}) async-start(), calls=%async_computation.3 | async-start | bytes 2097152 | tf_op jit(solution)/shard_map/psum | solution.py:14
  359.7 10.0 %copy-start.1 = (f32[1,512,512]{1,2,0:T(8,128)S(1)}, f32[1,512,512]{1,2,0:T(8,128)}, u32[]{:S(2)}) copy-start(f32[1,512,512]{1,2,0:T(8,128)} %all-reduce.10.cloned.1.call-done) | copy-start | bytes 3145732
  366.5 302.4 %all-reduce.14.cloned.1.call-start = ((), (), s32[]{:S(2)}) async-start(), calls=%async_computation.4 | async-start | bytes 2097152 | tf_op jit(solution)/shard_map/psum | solution.py:14
  521.6 302.5 %all-reduce.16.cloned.1.call-start = ((), (), s32[]{:S(2)}) async-start(), calls=%async_computation.5 | async-start | bytes 2097152 | tf_op jit(solution)/shard_map/psum | solution.py:14
Sparse Core Ops, SparseCore 0:
  10.7 27.0 all-gather.1
Sparse Core Ops, SparseCore 1:
  41.2 167.2 all-reduce.7
  212.3 147.3 all-reduce.9
  366.6 147.2 all-reduce.11
  521.6 147.2 all-reduce.13
  676.8 147.2 all-reduce.15
where the time goes:
time: 842 us; the launch traced here: 841 us
  waiting for transfers between devices  730 us (87%)
  local copies, waits for them, and re-layouts  33.2 us (4%)
  between operations  25.6 us (3%)
  matrix products  20.7 us (2%)
  other arithmetic  18 us (2%)
  blocking collectives  13.3 us (2%)
    psum x4, waiting for transfers between devices, from_root(): return lax.psum(jnp.where(mine, shard, jnp.zeros_like(shard)), axis)  577 us
    psum x1, waiting for transfers between devices, per_device(): totals = lax.psum(terms, 'row')  152 us
  transfers between devices with their start and end apart: 6, of which 5 were waited for; matrix products, arithmetic and copies ran while one was open for 4% of the time, Pallas kernels for 0%

commit v1 on v0

--- a/solution.py
+++ b/solution.py
@@ -43,7 +43,9 @@
         (my_row * local_rows, jnp.zeros((), jnp.int32)),
     )
     terms = placed - dense.reshape(SEP_ROWS, sources)
-    totals = lax.psum(terms, "row")
+    totals = terms
+    for hop in (1, 2, 4, 8, 16):
+        totals = totals + lax.ppermute(totals, "row", [(dev, dev ^ hop) for dev in range(32)])
     inverse_row_block, lower_rows = (
         lax.all_gather(sep_inverse, "src", axis=0, tiled=True),
         lax.all_gather(sep_lower, "src", axis=0, tiled=True),

time: 842 us -> 1330 us (1.58)
  waiting for transfers between devices: 730 us -> 1190 us
  starting transfers between devices: 0.26 us -> 16.7 us
    ppermute x0 -> x5, waiting for transfers between devices: none -> 615 us  [per_device(): lax.ppermute(totals, 'row', [(dev, dev ^ hop) for dev in range(32)])]
    psum x1 -> x0, waiting for transfers between devices: 152 us -> none  [per_device(): totals = lax.psum(terms, 'row')]
    ppermute x0 -> x5, starting transfers between devices: none -> 16.5 us  [per_device(): lax.ppermute(totals, 'row', [(dev, dev ^ hop) for dev in range(32)])]
  transfers between devices with their start and end apart: 6 -> 10, of which waited for: 5 -> 9; matrix products, arithmetic and copies ran while one was open for 4% -> 1% of each run, Pallas kernels for 0% -> 0%
where the time goes in v1:
time: 1330 us
  waiting for transfers between devices  1190 us (89%)
  local copies, waits for them, and re-layouts  32.4 us (2%)
  other arithmetic  25.1 us (2%)
  between operations  24 us (2%)
  matrix products  19.4 us (1%)
  starting transfers between devices  16.7 us (1%)
  blocking collectives  13.5 us (1%)
    ppermute x5, waiting for transfers between devices, per_device(): lax.ppermute(totals, 'row', [(dev, dev ^ hop) for dev in range(32)])  615 us
    psum x4, waiting for transfers between devices, from_root(): return lax.psum(jnp.where(mine, shard, jnp.zeros_like(shard)), axis)  579 us
  transfers between devices with their start and end apart: 10, of which 9 were waited for; matrix products, arithmetic and copies ran while one was open for 1% of the time, Pallas kernels for 0%

profile of v1, /device:TPU:8, one launch (start us, length us, event | category | flops | bytes accessed | tf_op | source)
XLA Modules:
  0.0 1325.3 jit_solution(12672322021810233946)
XLA Ops:
  7.2 0.0 copy-start
  7.2 0.0 all-gather.2.cloned.1.call-start
  7.2 1.2 copy.16
  8.4 0.4 copy-done
  8.8 3.0 fusion.34
  11.8 0.0 copy-start.9
  11.8 1.3 copy-done.9
  13.1 2.7 fusion.2
  15.8 1.9 copy.18
  17.7 0.0 copy-done.8
  17.7 0.1 iota_compare_fusion
  17.8 2.9 select_reduce_fusion
  20.7 5.4 copy.23
  26.1 2.5 broadcast_in_dim.36
  28.6 1.8 dynamic_update_slice.3
  30.4 4.2 sub.15
  34.7 1.9 collective-permute-start
  36.6 90.6 %collective-permute-done = f32[2048,512]{0,1:T(8,128)S(1)} collective-permute-done((f32[2048,512]{0,1:T(8,128)S(1)}, f32[2048,512]{0,1:T(8,128)S(1)}, u32[]{:S(2)}, u32[]{:S(2)}) %collective-permute-start) | collective-permute-done | bytes 4194336 | tf_op jit(solution)/shard_map/ppermute | solution.py:48
  127.2 1.1 add.46
  128.2 3.0 collective-permute-start.1
  131.3 90.1 %collective-permute-done.1 = f32[2048,512]{0,1:T(8,128)S(1)} collective-permute-done((f32[2048,512]{0,1:T(8,128)S(1)}, f32[2048,512]{0,1:T(8,128)S(1)}, u32[]{:S(2)}, u32[]{:S(2)}) %collective-permute-start.1) | collective-permute-done | bytes 4194336 | tf_op jit(solution)/shard_map/ppermute | solution.py:48
  221.4 1.1 add.47
  222.5 2.0 collective-permute-start.2
  224.4 88.9 %collective-permute-done.2 = f32[2048,512]{0,1:T(8,128)S(1)} collective-permute-done((f32[2048,512]{0,1:T(8,128)S(1)}, f32[2048,512]{0,1:T(8,128)S(1)}, u32[]{:S(2)}, u32[]{:S(2)}) %collective-permute-start.2) | collective-permute-done | bytes 4194336 | tf_op jit(solution)/shard_map/ppermute | solution.py:48
  313.4 1.1 add.48
  314.4 0.0 copy-start.5
  314.5 0.0 copy-start.3
  314.5 3.4 collective-permute-start.3
  317.9 178.2 %collective-permute-done.3 = f32[2048,512]{0,1:T(8,128)S(1)} collective-permute-done((f32[2048,512]{0,1:T(8,128)S(1)}, f32[2048,512]{0,1:T(8,128)S(1)}, u32[]{:S(2)}, u32[]{:S(2)}) %collective-permute-start.3) | collective-permute-done | bytes 4194336 | tf_op jit(solution)/shard_map/ppermute | solution.py:48
  496.1 2.7 add.49
  498.8 6.2 collective-permute-start.4
  505.0 0.0 all-gather.2.cloned.1.call-update
  505.0 0.0 all-reduce.7.cloned.1.call-start
  505.1 0.6 fusion.58
  506.3 13.5 %all_gather.7 = bf16[512,512]{1,0:T(8,128)(2,1)S(1)} all-gather(bf16[64,512]{1,0:T(8,128)(2,1)S(1)} %copy-done.3), channel_id=1, replica_groups=mesh['row'=32,'src'=8] {'src'}, dimensions={0}, use_global_device_ids=true | all-gather | bytes 589824 | tf_op jit(solution)/shard_map/all_gather | solution.py:50
  519.8 166.8 %collective-permute-done.4 = f32[2048,512]{0,1:T(8,128)} collective-permute-done((f32[2048,512]{0,1:T(8,128)}, f32[2048,512]{0,1:T(8,128)}, u32[]{:S(2)}, u32[]{:S(2)}) %collective-permute-start.4) | collective-permute-done | bytes 4194336 | tf_op jit(solution)/shard_map/ppermute | solution.py:48
  686.6 6.5 add.50
  693.1 3.8 fusion.8
  696.9 0.0 all-reduce.7.cloned.1.call-update
  696.9 0.0 all-reduce.9.cloned.1.call-start
  696.9 0.0 copy-done.4
  697.0 0.7 fusion.57
  700.9 145.0 %all-reduce.7.cloned.1.call-done = f32[1,512,512]{1,2,0:T(8,128)} async-done(((f32[1,512,512]{1,2,0:T(8,128)}), f32[1,512,512]{1,2,0:T(8,128)}) %all-reduce.7.cloned.1.call-update) | async-done | bytes 1048592 | tf_op jit(solution)/shard_map/psum | solution.py:14
  845.9 1.8 fusion.48
  847.7 3.5 fusion.7
  851.3 0.0 all-reduce.9.cloned.1.call-update
  851.3 0.0 all-reduce.11.cloned.1.call-start
  854.6 0.0 copy-done.2
  854.6 2.6 scatter.14
  857.2 141.9 %all-reduce.9.cloned.1.call-done = f32[1,512,512]{1,2,0:T(8,128)} async-done(((f32[1,512,512]{1,2,0:T(8,128)}), f32[1,512,512]{1,2,0:T(8,128)}) %all-reduce.9.cloned.1.call-update) | async-done | bytes 1048592 | tf_op jit(solution)/shard_map/psum | solution.py:14
  999.1 2.3 constant_dynamic-update-slice_fusion.2
  1001.4 1.8 fusion.42
  1003.2 3.2 fusion.6
  1006.4 0.0 all-reduce.11.cloned.1.call-update
  1006.4 0.0 all-reduce.13.cloned.1.call-start
  1009.5 144.7 %all-reduce.11.cloned.1.call-done = f32[1,512,512]{1,2,0:T(8,128)} async-done(((f32[1,512,512]{1,2,0:T(8,128)}), f32[1,512,512]{1,2,0:T(8,128)}) %all-reduce.11.cloned.1.call-update) | async-done | bytes 1048592 | tf_op jit(solution)/shard_map/psum | solution.py:14
  1154.2 2.3 constant_dynamic-update-slice_fusion.1
  1156.6 1.8 fusion.44
  1158.4 3.2 fusion.5
  1161.6 0.0 all-reduce.13.cloned.1.call-update
  1161.6 147.8 %all-reduce.13.cloned.1.call-done = f32[1,512,512]{1,2,0:T(8,128)} async-done(((f32[1,512,512]{1,2,0:T(8,128)}), f32[1,512,512]{1,2,0:T(8,128)}) %all-reduce.13.cloned.1.call-update) | async-done | bytes 1048592 | tf_op jit(solution)/shard_map/psum | solution.py:14
  1309.4 2.5 constant_dynamic-update-slice_fusion
  1311.9 5.2 copy.20
  1317.2 1.6 constant_dynamic-slice_fusion
  (14 shorter events, 0.0 us)
Async XLA Ops:
  7.2 1.7 copy-start
  7.2 685.9 %all-gather.2.cloned.1.call-start = ((), (), s32[]{:S(2)}) async-start(), calls=%async_computation | async-start | bytes 1179648 | tf_op jit(solution)/shard_map/all_gather | solution.py:51
  8.8 4.3 copy-start.6
  11.8 1.3 copy-start.9
  13.1 4.6 copy-start.8
  34.7 92.5 %collective-permute-start = (f32[2048,512]{0,1:T(8,128)S(1)}, f32[2048,512]{0,1:T(8,128)S(1)}, u32[]{:S(2)}, u32[]{:S(2)}) collective-permute-start(f32[2048,512]{0,1:T(8,128)S(1)} %sub.15), channel_id=1, source_target_pairs={{0,8},{8,0},{16,24},{24,16},{32,40},{40,32},{48,56},{56,48},{64,72... | collective-permute-start | bytes 12582920 | tf_op jit(solution)/shard_map/ppermute | solution.py:48
  128.2 93.1 %collective-permute-start.1 = (f32[2048,512]{0,1:T(8,128)S(1)}, f32[2048,512]{0,1:T(8,128)S(1)}, u32[]{:S(2)}, u32[]{:S(2)}) collective-permute-start(f32[2048,512]{0,1:T(8,128)S(1)} %add.46), channel_id=1, source_target_pairs={{0,16},{8,24},{16,0},{24,8},{32,48},{40,56},{48,32},{56,40},{64,80... | collective-permute-start | bytes 12582920 | tf_op jit(solution)/shard_map/ppermute | solution.py:48
  222.5 90.9 %collective-permute-start.2 = (f32[2048,512]{0,1:T(8,128)S(1)}, f32[2048,512]{0,1:T(8,128)S(1)}, u32[]{:S(2)}, u32[]{:S(2)}) collective-permute-start(f32[2048,512]{0,1:T(8,128)S(1)} %add.47), channel_id=1, source_target_pairs={{0,32},{8,40},{16,48},{24,56},{32,0},{40,8},{48,16},{56,24},{64,96... | collective-permute-start | bytes 12582920 | tf_op jit(solution)/shard_map/ppermute | solution.py:48
  314.4 190.6 %copy-start.5 = (s32[4]{0:T(128)S(1)}, s32[4]{0:T(128)}, u32[]{:S(2)}) copy-start(s32[4]{0:T(128)} %param.24) | copy-start | bytes 52
  314.5 191.8 %copy-start.3 = (bf16[64,512]{1,0:T(8,128)(2,1)S(1)}, bf16[64,512]{1,0:T(8,128)(2,1)}, u32[]{:S(2)}) copy-start(bf16[64,512]{1,0:T(8,128)(2,1)} %param.22) | copy-start | bytes 196612
  314.5 181.6 %collective-permute-start.3 = (f32[2048,512]{0,1:T(8,128)S(1)}, f32[2048,512]{0,1:T(8,128)S(1)}, u32[]{:S(2)}, u32[]{:S(2)}) collective-permute-start(f32[2048,512]{0,1:T(8,128)S(1)} %add.48), channel_id=1, source_target_pairs={{0,64},{8,72},{16,80},{24,88},{32,96},{40,104},{48,112},{56,120},{... | collective-permute-start | bytes 12582920 | tf_op jit(solution)/shard_map/ppermute | solution.py:48
  498.8 187.8 %collective-permute-start.4 = (f32[2048,512]{0,1:T(8,128)}, f32[2048,512]{0,1:T(8,128)}, u32[]{:S(2)}, u32[]{:S(2)}) collective-permute-start(f32[2048,512]{0,1:T(8,128)} %add.49), channel_id=1, source_target_pairs={{0,128},{8,136},{16,144},{24,152},{32,160},{40,168},{48,176},{56,1... | collective-permute-start | bytes 12582920 | tf_op jit(solution)/shard_map/ppermute | solution.py:48
  505.0 340.9 %all-reduce.7.cloned.1.call-start = ((), (), s32[]{:S(2)}) async-start(), calls=%async_computation.1 | async-start | bytes 2097152 | tf_op jit(solution)/shard_map/psum | solution.py:14
  693.1 3.9 copy-start.4
  696.9 302.2 %all-reduce.9.cloned.1.call-start = ((), (), s32[]{:S(2)}) async-start(), calls=%async_computation.2 | async-start | bytes 2097152 | tf_op jit(solution)/shard_map/psum | solution.py:14
  845.9 8.7 copy-start.2
  851.3 302.9 %all-reduce.11.cloned.1.call-start = ((), (), s32[]{:S(2)}) async-start(), calls=%async_computation.3 | async-start | bytes 2097152 | tf_op jit(solution)/shard_map/psum | solution.py:14
  854.6 148.6 %copy-start.7 = (bf16[512,1024]{1,0:T(8,128)(2,1)S(1)}, bf16[512,1024]{1,0:T(8,128)(2,1)}, u32[]{:S(2)}) copy-start(bf16[512,1024]{1,0:T(8,128)(2,1)} %all-gather.2.cloned.1.call-done) | copy-start | bytes 3145732
  1006.4 303.0 %all-reduce.13.cloned.1.call-start = ((), (), s32[]{:S(2)}) async-start(), calls=%async_computation.4 | async-start | bytes 2097152 | tf_op jit(solution)/shard_map/psum | solution.py:14
  1309.4 9.3 copy-start.1
Sparse Core Ops, SparseCore 0:
  505.2 21.5 all-gather.1
  697.0 148.8 all-reduce.6
  851.4 147.6 all-reduce.8
  1006.6 147.6 all-reduce.10
  1161.8 147.6 all-reduce.12
